TPU v7x, 256 devices: a whole 4x4x8 slice. The times are simulated.
256 devices in a mesh: band: 16 (over z, y_lo), pw: 16 (over x, y_hi, core).
Axes of the slice: x: 4, y: 4 (y_hi: 2, y_lo: 2; y = y_hi * 2 + y_lo), z: 8, core: 2. Of those that a mesh axis runs over, the one named last changes fastest.
Arguments:
- orbitals: bfloat16 [32, 192, 192, 256], P('band', 'pw'), may hold values from -5 to 5
- owner_group: int32 [1], replicated, may hold values from 0 to 15
Outputs:
- exchange_rows: float32 [32, 192, 192, 256], P('band', 'pw')
- owner_update: float32 [1, 192, 192, 256], P(None, 'pw', 'band')
All inputs are finite; a program needn't handle non-finite values.
Results may differ from a plain program's by a relative error of at most 0.0003.
Values may be sent and summed in bfloat16 or wider, within the bound.
A program may use at most 128 MiB of HBM per device.

v0:
```python
import math
import jax
import jax.numpy as jnp
from jax import lax
from jax.sharding import PartitionSpec as P

NX = 192
NY = 192
NZ = 256
SENT = 1
exact_share = 0.25
spacing = 0.2
highest = lax.Precision.HIGHEST


def broadcast(block, axis, owner):
    block = jnp.where(lax.axis_index(axis) == owner, block, jnp.zeros_like(block))
    return lax.psum(block, axis)


def dft_tables(length, number):
    samples = jnp.arange(length, dtype=jnp.int32)
    frequency = jnp.arange(number, dtype=jnp.int32)
    phase_index = samples[:, None] * frequency[None, :] % length
    phase_angle = phase_index.astype(jnp.float32) * (2 * math.pi / length)
    return (jnp.cos(phase_angle), jnp.sin(phase_angle))


def alternating(length):
    samples = jnp.arange(length, dtype=jnp.int32)
    return (1 - 2 * (samples % 2)).astype(jnp.float32)


def coulomb_table(ky_first, rows_y):
    freq_x = jnp.arange(NX, dtype=jnp.int32)
    freq_x = jnp.where(freq_x > NX // 2, freq_x - NX, freq_x)
    freq_y = ky_first + jnp.arange(rows_y, dtype=jnp.int32)
    freq_y = jnp.where(freq_y > NY // 2, freq_y - NY, freq_y)
    freq_z = jnp.arange(NZ // 2 + 1, dtype=jnp.int32)
    wave_x = freq_x.astype(jnp.float32) * (2 * math.pi / (NX * spacing))
    wave_y = freq_y.astype(jnp.float32) * (2 * math.pi / (NY * spacing))
    wave_z = freq_z.astype(jnp.float32) * (2 * math.pi / (NZ * spacing))
    square = (
        (wave_x * wave_x)[:, None, None]
        + (wave_y * wave_y)[None, :, None]
        + (wave_z * wave_z)[None, None, :]
    )
    safe = jnp.where(square > 0, square, 1.0)
    return jnp.where(square > 0, 4 * math.pi / safe, 0.0)


def complex_pass(spectrum, cosine_table, sine_table, pattern, direction):
    half_width = spectrum.shape[-1] // 2
    with_cosine = jnp.einsum(pattern, cosine_table, spectrum, precision=highest)
    with_sine = jnp.einsum(pattern, sine_table, spectrum, precision=highest)
    real_part = with_cosine[..., :half_width] + direction * with_sine[..., half_width:]
    imag_part = with_cosine[..., half_width:] - direction * with_sine[..., :half_width]
    return jnp.concatenate([real_part, imag_part], -1)


def split_pass(real_in, imag_in, cosine_table, sine_table, pattern, direction):
    real_part = jnp.einsum(
        pattern, cosine_table, real_in, precision=highest
    ) + direction * jnp.einsum(pattern, sine_table, imag_in, precision=highest)
    imag_part = jnp.einsum(
        pattern, cosine_table, imag_in, precision=highest
    ) - direction * jnp.einsum(pattern, sine_table, real_in, precision=highest)
    return (real_part, imag_part)


def forward_planes(density):
    cosine_z, sine_z = dft_tables(NZ, NZ // 2)
    z_table = jnp.concatenate([cosine_z, -sine_z], 1)
    spectrum = jnp.einsum("pxyz,zc->pxyc", density, z_table, precision=highest)
    nyquist = jnp.einsum("pxyz,z->pxy", density, alternating(NZ), precision=highest)
    cosine_y, sine_y = dft_tables(NY, NY)
    spectrum = complex_pass(spectrum, cosine_y, sine_y, "uy,pxyc->pxuc", 1.0)
    nyq_real, nyq_imag = split_pass(
        nyquist, jnp.zeros_like(nyquist), cosine_y, sine_y, "uy,pxy->pxu", 1.0
    )
    return (spectrum, nyq_real, nyq_imag)


def column_work(columns, nyq_real, nyq_imag, ky_first, rows_y):
    cosine_x, sine_x = dft_tables(NX, NX)
    spectrum = complex_pass(columns, cosine_x, sine_x, "ux,pxyc->puyc", 1.0)
    nyq_real, nyq_imag = split_pass(nyq_real, nyq_imag, cosine_x, sine_x, "ux,pxy->puy", 1.0)
    kernel = coulomb_table(ky_first, rows_y)
    main_kernel = kernel[:, :, : NZ // 2]
    edge_kernel = kernel[:, :, NZ // 2][None]
    spectrum = spectrum * jnp.concatenate([main_kernel, main_kernel], -1)[None]
    spectrum = complex_pass(spectrum, cosine_x, sine_x, "ux,pxyc->puyc", -1.0)
    nyq_real, nyq_imag = split_pass(
        nyq_real * edge_kernel, nyq_imag * edge_kernel, cosine_x, sine_x, "ux,pxy->puy", -1.0
    )
    return (spectrum, nyq_real, nyq_imag)


def inverse_planes(spectrum, nyq_real, nyq_imag):
    cosine_y, sine_y = dft_tables(NY, NY)
    spectrum = complex_pass(spectrum, cosine_y, sine_y, "uy,pxyc->pxuc", -1.0)
    edge_real, edge_imag = split_pass(nyq_real, nyq_imag, cosine_y, sine_y, "uy,pxy->pxu", -1.0)
    frequency = jnp.arange(NZ // 2, dtype=jnp.int32)
    cosine_z, sine_z = dft_tables(NZ, NZ // 2)
    first = frequency == 0
    real_weight = jnp.where(first, 1.0, 2.0).astype(jnp.float32)
    imag_weight = jnp.where(first, 0.0, 2.0).astype(jnp.float32)
    z_table = jnp.concatenate(
        [real_weight[:, None] * cosine_z.T, -imag_weight[:, None] * sine_z.T], 0
    )
    z_table = z_table * (1.0 / (NX * NY * NZ))
    result = jnp.einsum("pxyc,cz->pxyz", spectrum, z_table, precision=highest)
    edge_table = alternating(NZ) * (1.0 / (NX * NY * NZ))
    return result + edge_real[..., None] * edge_table


def on_device(orbitals, owner_group):
    own_count = orbitals.shape[0]
    slab_rows = orbitals.shape[1]
    received = broadcast(orbitals[:SENT], "band", owner_group[0])
    sent_values = received.astype(jnp.float32)
    own_values = orbitals.astype(jnp.float32)
    density = (own_values[:, None] * sent_values[None, :]).reshape(
        own_count * SENT, slab_rows, NY, NZ
    )
    planes, plane_real, plane_imag = forward_planes(density)
    rows_y = NY // lax.axis_size("pw")
    ky_first = lax.axis_index("pw") * rows_y
    pieces = []
    real_pieces = []
    imag_pieces = []
    for pair_index in range(planes.shape[0]):
        upper = pair_index + 1
        columns, col_real, col_imag = (
            lax.all_to_all(planes[pair_index:upper], "pw", split_axis=2, concat_axis=1, tiled=True),
            lax.all_to_all(
                plane_real[pair_index:upper], "pw", split_axis=2, concat_axis=1, tiled=True
            ),
            lax.all_to_all(
                plane_imag[pair_index:upper], "pw", split_axis=2, concat_axis=1, tiled=True
            ),
        )
        worked = column_work(columns, col_real, col_imag, ky_first, rows_y)
        main_back, real_back, imag_back = (
            lax.all_to_all(worked[0], "pw", split_axis=1, concat_axis=2, tiled=True),
            lax.all_to_all(worked[1], "pw", split_axis=1, concat_axis=2, tiled=True),
            lax.all_to_all(worked[2], "pw", split_axis=1, concat_axis=2, tiled=True),
        )
        pieces.append(main_back)
        real_pieces.append(real_back)
        imag_pieces.append(imag_back)
    returned = jnp.concatenate(pieces, 0)
    back_real = jnp.concatenate(real_pieces, 0)
    back_imag = jnp.concatenate(imag_pieces, 0)
    potential = inverse_planes(returned, back_real, back_imag).reshape(
        own_count, SENT, slab_rows, NY, NZ
    )
    exchange_rows = -exact_share * jnp.sum(potential * sent_values[None], 1)
    partial_value = -exact_share * jnp.sum(potential * own_values[:, None], 0)
    owner_update = lax.psum_scatter(partial_value, "band", scatter_dimension=2, tiled=True)
    return (exchange_rows, owner_update)


def solution(mesh):
    placed = (P("band", "pw", None, None), P())
    return jax.shard_map(
        on_device,
        mesh=mesh,
        in_specs=placed,
        out_specs=(P("band", "pw", None, None), P(None, "pw", "band", None)),
        check_vma=False,
    )
```

profile of v0, /device:TPU:6, one launch (start us, length us, event | category | flops | bytes accessed | tf_op | source)
XLA Modules:
  0.0 574.0 jit_solution(14537349176392429986)
XLA Ops:
  13.9 140.9 %all-reduce.2.cloned.1.call-done = bf16[12,192,256]{2,1,0:T(8,128)(2,1)} async-done(((bf16[12,192,256]{2,1,0:T(8,128)(2,1)}), bf16[12,192,256]{2,1,0:T(8,128)(2,1)}) %all-reduce.2.cloned.1.call-update) | async-done | bytes 1179664 | tf_op jit(solution)/shard_map/psum | solution.py:18
  156.3 5.5 fusion.1
  161.9 7.6 %convolution_bitcast_fusion.2 = f32[2,12,192,256]{3,2,1,0:T(8,128)} fusion(f32[2,12,192,256]{3,2,1,0:T(8,128)S(1)} %fusion.1), kind=kOutput, calls=%fused_computation.37 | convolution fusion | flops 2718240768 | bytes 9437184 | tf_op jit(solution)/shard_map/uy,pxyc->pxuc/dot_general | solution.py:55
  169.4 7.7 %convolution_bitcast_fusion.3 = f32[2,12,192,256]{3,2,1,0:T(8,128)} fusion(f32[2,12,192,256]{3,2,1,0:T(8,128)S(1)} %fusion.1), kind=kOutput, calls=%fused_computation.38 | convolution fusion | flops 2718240768 | bytes 9437184 | tf_op jit(solution)/shard_map/uy,pxyc->pxuc/dot_general | solution.py:54
  186.9 7.0 %all-to-all-start.4 = ((f32[16,1,144]{2,1,0:T(1,128)}), f32[16,1,144]{2,1,0:T(1,128)S(1)}, u32[]{:S(2)}, u32[]{:S(2)}) async-start(f32[16,1,144]{2,1,0:T(1,128)} %reshape.293), calls=%async_computation.4 | async-start | bytes 32768 | tf_op jit(solution)/shard_map/all_to_all | solution.py:136
  193.8 7.0 %slice_subtract_fusion = (f32[2,12,192,128]{3,2,1,0:T(8,128)}, f32[2,12,192,128]{3,2,1,0:T(8,128)}) fusion(f32[2,12,192,256]{3,2,1,0:T(8,128)} %convolution_bitcast_fusion.2, f32[2,12,192,256]{3,2,1,0:T(8,128)} %convolution_bitcast_fusion.3), kind=kLoop, calls=%fused_computation.23 | loop fusion | flops 1179648 | bytes 14155776 | tf_op jit(solution)/shard_map/sub | solution.py:57
  206.0 7.2 %all-to-all-start.5 = ((f32[16,1,144]{2,1,0:T(1,128)}), f32[16,1,144]{2,1,0:T(1,128)S(1)}, u32[]{:S(2)}, u32[]{:S(2)}) async-start(f32[16,1,144]{2,1,0:T(1,128)} %reshape.295), calls=%async_computation.5 | async-start | bytes 32768 | tf_op jit(solution)/shard_map/all_to_all | solution.py:139
  218.9 5.4 all-to-all-start.7
  229.9 6.0 %all-to-all-start.8 = ((f32[16,1,144]{2,1,0:T(1,128)}), f32[16,1,144]{2,1,0:T(1,128)S(1)}, u32[]{:S(2)}, u32[]{:S(2)}) async-start(f32[16,1,144]{2,1,0:T(1,128)} %reshape.289), calls=%async_computation.8 | async-start | bytes 32768 | tf_op jit(solution)/shard_map/all_to_all | solution.py:139
  254.7 5.7 all-to-all-start.9
  265.9 5.5 all-to-all-start.11
  277.0 5.5 all-to-all-start.10
  288.0 5.5 all-to-all-start.6
  302.0 7.2 %all-to-all-start.2 = ((f32[1,12,192,256]{3,0,1,2:T(1,128)}), f32[1,12,192,256]{3,0,1,2:T(1,128)}, u32[]{:S(2)}, u32[]{:S(2)}) async-start(f32[1,12,192,256]{3,0,1,2:T(1,128)} %copy.86), calls=%async_computation.2 | async-start | bytes 4718592 | tf_op jit(solution)/shard_map/all_to_all | solution.py:135
  309.2 5.5 copy.81
  314.7 24.4 %all-to-all-done.2 = f32[1,12,192,256]{3,0,1,2:T(1,128)} async-done(((f32[1,12,192,256]{3,0,1,2:T(1,128)}), f32[1,12,192,256]{3,0,1,2:T(1,128)}, u32[]{:S(2)}, u32[]{:S(2)}) %all-to-all-start.2) | async-done | bytes 2359328 | tf_op jit(solution)/shard_map/all_to_all | solution.py:135
  339.1 7.9 %all-to-all-start = ((f32[1,12,192,256]{3,0,1,2:T(1,128)}), f32[1,12,192,256]{3,0,1,2:T(1,128)}, u32[]{:S(2)}, u32[]{:S(2)}) async-start(f32[1,12,192,256]{3,0,1,2:T(1,128)} %copy.81), calls=%async_computation | async-start | bytes 4718592 | tf_op jit(solution)/shard_map/all_to_all | solution.py:135
  378.7 7.2 %all-to-all-start.3 = ((f32[1,192,12,256]{3,0,2,1:T(1,128)}), f32[1,192,12,256]{3,0,2,1:T(1,128)}, u32[]{:S(2)}, u32[]{:S(2)}) async-start(f32[1,192,12,256]{3,0,2,1:T(1,128)} %copy.89), calls=%async_computation.3 | async-start | bytes 4718592 | tf_op jit(solution)/shard_map/all_to_all | solution.py:145
  416.2 7.5 %all-to-all-start.1 = ((f32[1,192,12,256]{3,0,2,1:T(1,128)}), f32[1,192,12,256]{3,0,2,1:T(1,128)}, u32[]{:S(2)}, u32[]{:S(2)}) async-start(f32[1,192,12,256]{3,0,2,1:T(1,128)} %copy.84), calls=%async_computation.1 | async-start | bytes 4718592 | tf_op jit(solution)/shard_map/all_to_all | solution.py:145
  437.4 16.2 %all-to-all-done.1 = f32[1,192,12,256]{3,0,2,1:T(1,128)} async-done(((f32[1,192,12,256]{3,0,2,1:T(1,128)}), f32[1,192,12,256]{3,0,2,1:T(1,128)}, u32[]{:S(2)}, u32[]{:S(2)}) %all-to-all-start.1) | async-done | bytes 2359328 | tf_op jit(solution)/shard_map/all_to_all | solution.py:145
  459.4 5.8 %convolution_bitcast_fusion = f32[2,12,192,256]{3,2,1,0:T(8,128)S(1)} fusion(f32[2,12,192,256]{3,2,1,0:T(8,128)S(1)} %copy_dynamic-update-slice_fusion), kind=kOutput, calls=%fused_computation.35 | convolution fusion | flops 2718240768 | bytes 9437184 | tf_op jit(solution)/shard_map/uy,pxyc->pxuc/dot_general | solution.py:55
  465.3 5.6 convolution_bitcast_fusion.1
  472.5 6.4 %fusion.2 = (f32[12,192,256]{2,1,0:T(8,128)S(1)}, f32[2,12,192,256]{3,2,1,0:T(8,128)}) fusion(bf16[2,12,192,256]{3,2,1,0:T(8,128)(2,1)S(1)} %copy-done.1, f32[256]{0:T(256)S(1)} %broadcast_multiply_fusion, f32[2,12,192]{2,1,0:T(8,128)S(1)} %fusion.23, f32[12,192,256]{2,1,0:T(8,128)S(1)} %mul.580, f32[128,256]{1,0:T(8,128)S(1)} %get-tuple-element.28, ...), kind=kOutput, calls=%fused_computation.4 | convolution fusion | flops 3632857088 | bytes 16796672 | tf_op jit(solution)/shard_map/pxyc,cz->pxyz/dot_general | solution.py:112
  482.2 83.0 %reduce-scatter.2.cloned.1.call-done = f32[1,12,12,256]{3,1,0,2:T(8,128)} async-done(((f32[1,12,192,256]{3,1,0,2:T(8,128)}), f32[1,12,12,256]{3,1,0,2:T(8,128)}) %reduce-scatter.2.cloned.1.call-update) | async-done | bytes 147472 | tf_op jit(solution)/shard_map/reduce_scatter | solution.py:160
  (183 shorter events, 165.2 us)
Async XLA Ops:
  7.2 147.6 %all-reduce.2.cloned.1.call-start = ((), (), s32[]{:S(2)}) async-start(), calls=%async_computation.13 | async-start | bytes 2359296 | tf_op jit(solution)/shard_map/psum | solution.py:18
  169.4 7.7 %copy-start = (bf16[2,12,192,256]{3,2,1,0:T(8,128)(2,1)S(1)}, bf16[2,12,192,256]{3,2,1,0:T(8,128)(2,1)}, u32[]{:S(2)}) copy-start(bf16[2,12,192,256]{3,2,1,0:T(8,128)(2,1)} %param.2) | copy-start | bytes 7077892
  186.9 19.2 %all-to-all-start.4 = ((f32[16,1,144]{2,1,0:T(1,128)}), f32[16,1,144]{2,1,0:T(1,128)S(1)}, u32[]{:S(2)}, u32[]{:S(2)}) async-start(f32[16,1,144]{2,1,0:T(1,128)} %reshape.293), calls=%async_computation.4 | async-start | bytes 32768 | tf_op jit(solution)/shard_map/all_to_all | solution.py:136
  206.0 12.8 %all-to-all-start.5 = ((f32[16,1,144]{2,1,0:T(1,128)}), f32[16,1,144]{2,1,0:T(1,128)S(1)}, u32[]{:S(2)}, u32[]{:S(2)}) async-start(f32[16,1,144]{2,1,0:T(1,128)} %reshape.295), calls=%async_computation.5 | async-start | bytes 32768 | tf_op jit(solution)/shard_map/all_to_all | solution.py:139
  218.9 11.0 %all-to-all-start.7 = ((f32[16,1,144]{2,1,0:T(1,128)}), f32[16,1,144]{2,1,0:T(1,128)S(1)}, u32[]{:S(2)}, u32[]{:S(2)}) async-start(f32[16,1,144]{2,1,0:T(1,128)} %reshape.287), calls=%async_computation.7 | async-start | bytes 32768 | tf_op jit(solution)/shard_map/all_to_all | solution.py:136
  229.9 11.5 %all-to-all-start.8 = ((f32[16,1,144]{2,1,0:T(1,128)}), f32[16,1,144]{2,1,0:T(1,128)S(1)}, u32[]{:S(2)}, u32[]{:S(2)}) async-start(f32[16,1,144]{2,1,0:T(1,128)} %reshape.289), calls=%async_computation.8 | async-start | bytes 32768 | tf_op jit(solution)/shard_map/all_to_all | solution.py:139
  254.7 11.2 %all-to-all-start.9 = ((f32[16,1,144]{2,1,0:T(1,128)}), f32[16,1,144]{2,1,0:T(1,128)S(1)}, u32[]{:S(2)}, u32[]{:S(2)}) async-start(f32[16,1,144]{2,1,0:T(1,128)} %reshape.291), calls=%async_computation.9 | async-start | bytes 32768 | tf_op jit(solution)/shard_map/all_to_all | solution.py:146
  265.9 11.0 %all-to-all-start.11 = ((f32[16,1,144]{2,1,0:T(1,128)}), f32[16,1,144]{2,1,0:T(1,128)S(1)}, u32[]{:S(2)}, u32[]{:S(2)}) async-start(f32[16,1,144]{2,1,0:T(1,128)} %reshape.299), calls=%async_computation.11 | async-start | bytes 32768 | tf_op jit(solution)/shard_map/all_to_all | solution.py:147
  277.0 20.6 %copy-start.6 = (f32[16,1,144]{2,1,0:T(1,128)}, f32[16,1,144]{2,1,0:T(1,128)S(1)}, u32[]{:S(2)}) copy-start(f32[16,1,144]{2,1,0:T(1,128)S(1)} %all-to-all-done.11) | copy-start | bytes 27652
  277.0 11.0 %all-to-all-start.10 = ((f32[16,1,144]{2,1,0:T(1,128)}), f32[16,1,144]{2,1,0:T(1,128)S(1)}, u32[]{:S(2)}, u32[]{:S(2)}) async-start(f32[16,1,144]{2,1,0:T(1,128)} %reshape.301), calls=%async_computation.10 | async-start | bytes 32768 | tf_op jit(solution)/shard_map/all_to_all | solution.py:147
  288.0 9.6 %copy-start.8 = (f32[16,1,144]{2,1,0:T(1,128)}, f32[16,1,144]{2,1,0:T(1,128)S(1)}, u32[]{:S(2)}) copy-start(f32[16,1,144]{2,1,0:T(1,128)S(1)} %all-to-all-done.10) | copy-start | bytes 27652
  288.0 13.4 %all-to-all-start.6 = ((f32[16,1,144]{2,1,0:T(1,128)}), f32[16,1,144]{2,1,0:T(1,128)S(1)}, u32[]{:S(2)}, u32[]{:S(2)}) async-start(f32[16,1,144]{2,1,0:T(1,128)} %reshape.297), calls=%async_computation.6 | async-start | bytes 32768 | tf_op jit(solution)/shard_map/all_to_all | solution.py:146
  302.0 37.1 %all-to-all-start.2 = ((f32[1,12,192,256]{3,0,1,2:T(1,128)}), f32[1,12,192,256]{3,0,1,2:T(1,128)}, u32[]{:S(2)}, u32[]{:S(2)}) async-start(f32[1,12,192,256]{3,0,1,2:T(1,128)} %copy.86), calls=%async_computation.2 | async-start | bytes 4718592 | tf_op jit(solution)/shard_map/all_to_all | solution.py:135
  339.1 39.6 %all-to-all-start = ((f32[1,12,192,256]{3,0,1,2:T(1,128)}), f32[1,12,192,256]{3,0,1,2:T(1,128)}, u32[]{:S(2)}, u32[]{:S(2)}) async-start(f32[1,12,192,256]{3,0,1,2:T(1,128)} %copy.81), calls=%async_computation | async-start | bytes 4718592 | tf_op jit(solution)/shard_map/all_to_all | solution.py:135
  359.5 4.9 copy-start.2
  378.7 37.5 %all-to-all-start.3 = ((f32[1,192,12,256]{3,0,2,1:T(1,128)}), f32[1,192,12,256]{3,0,2,1:T(1,128)}, u32[]{:S(2)}, u32[]{:S(2)}) async-start(f32[1,192,12,256]{3,0,2,1:T(1,128)} %copy.89), calls=%async_computation.3 | async-start | bytes 4718592 | tf_op jit(solution)/shard_map/all_to_all | solution.py:145
  397.0 4.9 copy-start.3
  416.2 9.5 %copy-start.7 = (f32[16,1,144]{2,1,0:T(1,128)S(1)}, f32[16,1,144]{2,1,0:T(1,128)}, u32[]{:S(2)}) copy-start(f32[16,1,144]{2,1,0:T(1,128)} %copy-done.6) | copy-start | bytes 27652
  416.2 10.9 %copy-start.9 = (f32[16,1,144]{2,1,0:T(1,128)S(1)}, f32[16,1,144]{2,1,0:T(1,128)}, u32[]{:S(2)}) copy-start(f32[16,1,144]{2,1,0:T(1,128)} %copy-done.8) | copy-start | bytes 27652
  416.2 12.3 %copy-start.11 = (f32[16,1,144]{2,1,0:T(1,128)S(1)}, f32[16,1,144]{2,1,0:T(1,128)}, u32[]{:S(2)}) copy-start(f32[16,1,144]{2,1,0:T(1,128)} %copy-done.10) | copy-start | bytes 27652
  416.2 37.4 %all-to-all-start.1 = ((f32[1,192,12,256]{3,0,2,1:T(1,128)}), f32[1,192,12,256]{3,0,2,1:T(1,128)}, u32[]{:S(2)}, u32[]{:S(2)}) async-start(f32[1,192,12,256]{3,0,2,1:T(1,128)} %copy.84), calls=%async_computation.1 | async-start | bytes 4718592 | tf_op jit(solution)/shard_map/all_to_all | solution.py:145
  423.7 141.5 %reduce-scatter.2.cloned.1.call-start = ((), (), s32[]{:S(2)}) async-start(), calls=%async_computation.14 | async-start | bytes 3342336 | tf_op jit(solution)/shard_map/reduce_scatter | solution.py:160
  457.5 1.7 copy-start.5
  470.8 1.7 copy-start.1
  (2 other events, 2.1 us)
Sparse Core Ops, SparseCore 0:
  11.2 143.5 all-reduce.1
  482.4 82.7 reduce-scatter.1
where the time goes:
time: 581 us; the launch traced here: 574 us
  waiting for transfers between devices  282 us (49%)
  matrix products  94.3 us (16%)
  starting transfers between devices  77.6 us (13%)
  local copies, waits for them, and re-layouts  72.4 us (12%)
  other arithmetic  31.5 us (5%)
  between operations  15.8 us (3%)
    psum x1, waiting for transfers between devices, broadcast(): return lax.psum(block, axis)  141 us
    reduce_scatter x1, waiting for transfers between devices, on_device(): lax.psum_scatter(partial_value, 'band', scatter_dimension=2, tiled=True)  83 us
    dot_general x6, matrix products, complex_pass(): with_sine = jnp.einsum(pattern, sine_table, spectrum, precision=highest)  29.3 us
    dot_general x6, matrix products, complex_pass(): with_cosine = jnp.einsum(pattern, cosine_table, spectrum, precision=highest)  26.4 us
    all_to_all x2, waiting for transfers between devices, on_device(): lax.all_to_all(planes[pair_index:upper], 'pw', split_axis=2, concat_axis=...  24.4 us
    all_to_all x2, waiting for transfers between devices, on_device(): lax.all_to_all(worked[0], 'pw', split_axis=1, concat_axis=2, tiled=True)  16.2 us
    all_to_all x2, starting transfers between devices, on_device(): lax.all_to_all(planes[pair_index:upper], 'pw', split_axis=2, concat_axis=...  15.1 us
    all_to_all x2, starting transfers between devices, on_device(): lax.all_to_all(worked[0], 'pw', split_axis=1, concat_axis=2, tiled=True)  14.7 us
  transfers between devices with their start and end apart: 14, of which 10 were waited for; matrix products, arithmetic and copies ran while one was open for 20% of the time, Pallas kernels for 0%

commit v1 on v0

--- a/solution.py
+++ b/solution.py
@@ -15,7 +15,7 @@
 
 def broadcast(block, axis, owner):
     block = jnp.where(lax.axis_index(axis) == owner, block, jnp.zeros_like(block))
-    return lax.psum(block, axis)
+    return jnp.sum(lax.all_gather(block, axis), axis=0)
 
 
 def dft_tables(length, number):

time: 581 us -> 844 us (1.45)
  waiting for transfers between devices: 282 us -> 532 us
  other arithmetic: 31.5 us -> 42.1 us
    all_gather x0 -> x1, waiting for transfers between devices: none -> 392 us  [broadcast(): return jnp.sum(lax.all_gather(block, axis), axis=0)]
    psum x1 -> x0, waiting for transfers between devices: 141 us -> none  [broadcast(): return lax.psum(block, axis)]
    reduce_sum x0 -> x1, other arithmetic: none -> 10.9 us  [broadcast(): return jnp.sum(lax.all_gather(block, axis), axis=0)]
  transfers between devices with their start and end apart: 14 -> 14, of which waited for: 10 -> 7; matrix products, arithmetic and copies ran while one was open for 20% -> 16% of each run, Pallas kernels for 0% -> 0%
where the time goes in v1:
time: 844 us; the launch traced here: 839 us
  waiting for transfers between devices  532 us (63%)
  matrix products  93 us (11%)
  starting transfers between devices  83.1 us (10%)
  local copies, waits for them, and re-layouts  73.1 us (9%)
  other arithmetic  42.1 us (5%)
  between operations  15.9 us (2%)
    all_gather x1, waiting for transfers between devices, broadcast(): return jnp.sum(lax.all_gather(block, axis), axis=0)  392 us
    reduce_scatter x1, waiting for transfers between devices, on_device(): lax.psum_scatter(partial_value, 'band', scatter_dimension=2, tiled=True)  90.2 us
    dot_general x6, matrix products, complex_pass(): with_sine = jnp.einsum(pattern, sine_table, spectrum, precision=highest)  29.6 us
    dot_general x6, matrix products, complex_pass(): with_cosine = jnp.einsum(pattern, cosine_table, spectrum, precision=highest)  25.9 us
    all_to_all x2, waiting for transfers between devices, on_device(): lax.all_to_all(planes[pair_index:upper], 'pw', split_axis=2, concat_axis=...  24.4 us
  transfers between devices with their start and end apart: 14, of which 7 were waited for; matrix products, arithmetic and copies ran while one was open for 16% of the time, Pallas kernels for 0%

profile of v1, /device:TPU:6, one launch (start us, length us, event | category | flops | bytes accessed | tf_op | source)
XLA Modules:
  0.0 838.7 jit_solution(3224417450145283547)
XLA Ops:
  14.8 391.6 %all-gather.3.cloned.1.call-done = bf16[16,12,192,256]{3,2,1,0:T(8,128)(2,1)} async-done(((bf16[1,12,192,256]{3,2,1,0:T(8,128)(2,1)}), bf16[16,12,192,256]{3,2,1,0:T(8,128)(2,1)}) %all-gather.3.cloned.1.call-update) | async-done | bytes 18874384 | tf_op jit(solution)/shard_map/all_gather | solution.py:18
  406.4 10.9 %reduce.4 = bf16[12,192,256]{2,1,0:T(8,128)(2,1)S(1)} reduce(bf16[16,12,192,256]{3,2,1,0:T(8,128)(2,1)} %all-gather.3.cloned.1.call-done, bf16[]{:T(256)} %constant.93.clone.1), dimensions={0}, to_apply=%region_0.1 | reduce | flops 8847360 | bytes 20054018 | tf_op jit(solution)/shard_map/reduce_sum | solution.py:18
  422.9 7.4 convolution_bitcast_fusion.2
  430.3 8.0 convolution_bitcast_fusion.3
  447.0 7.0 all-to-all-start.5
  455.0 6.9 slice_subtract_fusion
  467.1 7.2 all-to-all-start.4
  479.9 5.7 all-to-all-start.8
  491.1 7.2 all-to-all-start.7
  504.5 7.5 all-to-all-start.6
  521.3 7.2 all-to-all-start.9
  534.1 5.4 all-to-all-start.10
  545.2 5.9 all-to-all-start.11
  559.7 7.2 all-to-all-start.2
  566.9 5.5 copy.81
  572.4 24.4 %all-to-all-done.2 = f32[1,12,192,256]{3,0,1,2:T(1,128)} async-done(((f32[1,12,192,256]{3,0,1,2:T(1,128)}), f32[1,12,192,256]{3,0,1,2:T(1,128)}, u32[]{:S(2)}, u32[]{:S(2)}) %all-to-all-start.2) | async-done | bytes 2359328 | tf_op jit(solution)/shard_map/all_to_all | solution.py:135
  596.8 7.9 all-to-all-start
  636.1 7.2 all-to-all-start.3
  673.6 7.5 all-to-all-start.1
  694.7 16.3 %all-to-all-done.1 = f32[1,192,12,256]{3,0,2,1:T(1,128)} async-done(((f32[1,192,12,256]{3,0,2,1:T(1,128)}), f32[1,192,12,256]{3,0,2,1:T(1,128)}, u32[]{:S(2)}, u32[]{:S(2)}) %all-to-all-start.1) | async-done | bytes 2359328 | tf_op jit(solution)/shard_map/all_to_all | solution.py:145
  716.8 5.9 convolution_bitcast_fusion
  722.7 5.6 convolution_bitcast_fusion.1
  730.0 6.4 fusion.2
  739.7 90.2 %reduce-scatter.2.cloned.1.call-done = f32[1,12,12,256]{3,1,0,2:T(8,128)} async-done(((f32[1,12,192,256]{3,1,0,2:T(8,128)}), f32[1,12,12,256]{3,1,0,2:T(8,128)}) %reduce-scatter.2.cloned.1.call-update) | async-done | bytes 147472 | tf_op jit(solution)/shard_map/reduce_scatter | solution.py:160
  (196 shorter events, 160.8 us)
Async XLA Ops:
  7.2 399.2 %all-gather.3.cloned.1.call-start = ((), (), s32[]{:S(2)}) async-start(), calls=%async_computation.14 | async-start | bytes 20054016 | tf_op jit(solution)/shard_map/all_gather | solution.py:18
  14.3 392.1 %copy-start.4 = (f32[192,12,129]{2,0,1:T(8,128)}, f32[192,12,129]{2,0,1:T(8,128)S(1)}, u32[]{:S(2)}) copy-start(f32[192,12,129]{2,0,1:T(8,128)S(1)} %fusion.7) | copy-start | bytes 3566596
  14.8 475.3 %copy-start.14 = (f32[192,12]{0,1:T(8,128)}, f32[192,12]{0,1:T(8,128)S(1)}, u32[]{:S(2)}) copy-start(f32[192,12]{0,1:T(8,128)S(1)} %slice_reduce_fusion) | copy-start | bytes 27652
  430.3 8.0 copy-start.16
  438.3 5.4 copy-start.17
  447.0 20.1 %all-to-all-start.5 = ((f32[16,1,144]{2,1,0:T(1,128)}), f32[16,1,144]{2,1,0:T(1,128)S(1)}, u32[]{:S(2)}, u32[]{:S(2)}) async-start(f32[16,1,144]{2,1,0:T(1,128)} %reshape.302), calls=%async_computation.5 | async-start | bytes 32768 | tf_op jit(solution)/shard_map/all_to_all | solution.py:139
  467.1 12.8 %all-to-all-start.4 = ((f32[16,1,144]{2,1,0:T(1,128)}), f32[16,1,144]{2,1,0:T(1,128)S(1)}, u32[]{:S(2)}, u32[]{:S(2)}) async-start(f32[16,1,144]{2,1,0:T(1,128)} %reshape.300), calls=%async_computation.4 | async-start | bytes 32768 | tf_op jit(solution)/shard_map/all_to_all | solution.py:136
  479.9 11.2 %all-to-all-start.8 = ((f32[16,1,144]{2,1,0:T(1,128)}), f32[16,1,144]{2,1,0:T(1,128)S(1)}, u32[]{:S(2)}, u32[]{:S(2)}) async-start(f32[16,1,144]{2,1,0:T(1,128)} %reshape.296), calls=%async_computation.8 | async-start | bytes 32768 | tf_op jit(solution)/shard_map/all_to_all | solution.py:139
  491.1 23.3 %copy-start.15 = (f32[192,12]{0,1:T(8,128)S(1)}, f32[192,12]{0,1:T(8,128)}, u32[]{:S(2)}) copy-start(f32[192,12]{0,1:T(8,128)} %copy-done.14) | copy-start | bytes 27652
  491.1 13.4 %all-to-all-start.7 = ((f32[16,1,144]{2,1,0:T(1,128)}), f32[16,1,144]{2,1,0:T(1,128)S(1)}, u32[]{:S(2)}, u32[]{:S(2)}) async-start(f32[16,1,144]{2,1,0:T(1,128)} %reshape.294), calls=%async_computation.7 | async-start | bytes 32768 | tf_op jit(solution)/shard_map/all_to_all | solution.py:136
  504.5 16.8 %all-to-all-start.6 = ((f32[16,1,144]{2,1,0:T(1,128)}), f32[16,1,144]{2,1,0:T(1,128)S(1)}, u32[]{:S(2)}, u32[]{:S(2)}) async-start(f32[16,1,144]{2,1,0:T(1,128)} %reshape.304), calls=%async_computation.6 | async-start | bytes 32768 | tf_op jit(solution)/shard_map/all_to_all | solution.py:146
  521.3 12.8 %all-to-all-start.9 = ((f32[16,1,144]{2,1,0:T(1,128)}), f32[16,1,144]{2,1,0:T(1,128)S(1)}, u32[]{:S(2)}, u32[]{:S(2)}) async-start(f32[16,1,144]{2,1,0:T(1,128)} %reshape.298), calls=%async_computation.9 | async-start | bytes 32768 | tf_op jit(solution)/shard_map/all_to_all | solution.py:146
  534.1 21.1 %copy-start.8 = (f32[16,1,144]{2,1,0:T(1,128)}, f32[16,1,144]{2,1,0:T(1,128)S(1)}, u32[]{:S(2)}) copy-start(f32[16,1,144]{2,1,0:T(1,128)S(1)} %all-to-all-done.9) | copy-start | bytes 27652
  534.1 11.0 %all-to-all-start.10 = ((f32[16,1,144]{2,1,0:T(1,128)}), f32[16,1,144]{2,1,0:T(1,128)S(1)}, u32[]{:S(2)}, u32[]{:S(2)}) async-start(f32[16,1,144]{2,1,0:T(1,128)} %reshape.308), calls=%async_computation.10 | async-start | bytes 32768 | tf_op jit(solution)/shard_map/all_to_all | solution.py:147
  545.2 10.1 %copy-start.10 = (f32[16,1,144]{2,1,0:T(1,128)}, f32[16,1,144]{2,1,0:T(1,128)S(1)}, u32[]{:S(2)}) copy-start(f32[16,1,144]{2,1,0:T(1,128)S(1)} %all-to-all-done.10) | copy-start | bytes 27652
  545.2 13.9 %all-to-all-start.11 = ((f32[16,1,144]{2,1,0:T(1,128)}), f32[16,1,144]{2,1,0:T(1,128)S(1)}, u32[]{:S(2)}, u32[]{:S(2)}) async-start(f32[16,1,144]{2,1,0:T(1,128)} %reshape.306), calls=%async_computation.11 | async-start | bytes 32768 | tf_op jit(solution)/shard_map/all_to_all | solution.py:147
  559.7 37.1 %all-to-all-start.2 = ((f32[1,12,192,256]{3,0,1,2:T(1,128)}), f32[1,12,192,256]{3,0,1,2:T(1,128)}, u32[]{:S(2)}, u32[]{:S(2)}) async-start(f32[1,12,192,256]{3,0,1,2:T(1,128)} %copy.86), calls=%async_computation.2 | async-start | bytes 4718592 | tf_op jit(solution)/shard_map/all_to_all | solution.py:135
  596.8 39.3 %all-to-all-start = ((f32[1,12,192,256]{3,0,1,2:T(1,128)}), f32[1,12,192,256]{3,0,1,2:T(1,128)}, u32[]{:S(2)}, u32[]{:S(2)}) async-start(f32[1,12,192,256]{3,0,1,2:T(1,128)} %copy.81), calls=%async_computation | async-start | bytes 4718592 | tf_op jit(solution)/shard_map/all_to_all | solution.py:135
  636.1 37.5 %all-to-all-start.3 = ((f32[1,192,12,256]{3,0,2,1:T(1,128)}), f32[1,192,12,256]{3,0,2,1:T(1,128)}, u32[]{:S(2)}, u32[]{:S(2)}) async-start(f32[1,192,12,256]{3,0,2,1:T(1,128)} %copy.89), calls=%async_computation.3 | async-start | bytes 4718592 | tf_op jit(solution)/shard_map/all_to_all | solution.py:145
  673.6 9.5 %copy-start.9 = (f32[16,1,144]{2,1,0:T(1,128)S(1)}, f32[16,1,144]{2,1,0:T(1,128)}, u32[]{:S(2)}) copy-start(f32[16,1,144]{2,1,0:T(1,128)} %copy-done.8) | copy-start | bytes 27652
  673.6 10.9 %copy-start.11 = (f32[16,1,144]{2,1,0:T(1,128)S(1)}, f32[16,1,144]{2,1,0:T(1,128)}, u32[]{:S(2)}) copy-start(f32[16,1,144]{2,1,0:T(1,128)} %copy-done.10) | copy-start | bytes 27652
  673.6 12.3 %copy-start.13 = (f32[16,1,144]{2,1,0:T(1,128)S(1)}, f32[16,1,144]{2,1,0:T(1,128)}, u32[]{:S(2)}) copy-start(f32[16,1,144]{2,1,0:T(1,128)} %copy-done.12) | copy-start | bytes 27652
  673.6 37.4 %all-to-all-start.1 = ((f32[1,192,12,256]{3,0,2,1:T(1,128)}), f32[1,192,12,256]{3,0,2,1:T(1,128)}, u32[]{:S(2)}, u32[]{:S(2)}) async-start(f32[1,192,12,256]{3,0,2,1:T(1,128)} %copy.84), calls=%async_computation.1 | async-start | bytes 4718592 | tf_op jit(solution)/shard_map/all_to_all | solution.py:145
  681.1 148.8 %reduce-scatter.2.cloned.1.call-start = ((), (), s32[]{:S(2)}) async-start(), calls=%async_computation.13 | async-start | bytes 3342336 | tf_op jit(solution)/shard_map/reduce_scatter | solution.py:160
  (8 other events, 18.6 us)
Sparse Core Ops, SparseCore 0:
  10.4 395.9 all-gather.2
  739.8 90.0 reduce-scatter.1
